TPU v7x, 32 devices: a whole 2x2x4 slice. The times are simulated.
32 devices in a mesh: mem: 4 (over y, x), tile: 8 (over z, core).
Axes of the slice: x: 2, y: 2, z: 4, core: 2. Of those that a mesh axis runs over, the one named last changes fastest.
Arguments:
- perturbations: bfloat16 [96, 3, 32, 8192], P('mem', None, None, 'tile'), may hold values from -6 to 6
- member_weight: float32 [96], P('mem'), may hold values from 0.3 to 3
- innovation: float32 [3, 32, 8192], P(None, 'mem', 'tile'), may hold values from -6 to 6
- obs_weight: float32 [3, 32], P(None, 'mem'), may hold values from 0.1 to 1
- static_var: float32 [3, 32, 8192], P(None, 'mem', 'tile'), may hold values from 0.1 to 1
- obs_mask: int32 [8192], P('tile'), may hold values 0 or 1
- kernel_x: float32 [32, 5], replicated, may hold values from 0.1 to 0.5
- kernel_y: float32 [32, 5], replicated, may hold values from 0.1 to 0.5
Outputs:
- analysis: float32 [3, 32, 8192], P(None, 'mem', 'tile')
All inputs are finite; a program needn't handle non-finite values. No bound on the sum of `obs_mask` on one device may be relied on, other than what follows from the above.
Results may differ from a plain program's by a relative error of at most 0.0003.
Values sent between devices are 32-bit elements; how exact they have to be, the bound alone decides.
A program may use at most 64 MiB of HBM per device.

v0:
```python
import functools

import jax
import jax.numpy as jnp
import numpy as np
from jax import lax
from jax.experimental import pallas as pl
from jax.experimental.pallas import tpu as pltpu
from jax.sharding import PartitionSpec as P

TILE_X = 32
TILE_Y = 32
GRID_Y = 4
STEPS = 2
COARSE_X = TILE_X // 2
COARSE_Y = TILE_Y // 2
COARSE = COARSE_X * COARSE_Y
GROUP_LEVELS = 16
LANES = 256
MESH = pl.DeviceIdType.MESH
F32 = jnp.float32
BF16 = jnp.bfloat16


def interp_rows(fine_count):
    coarse_count = fine_count // 2
    rows = np.zeros((fine_count, coarse_count), np.float32)
    for i in range(fine_count):
        low = min(max((i - 1) // 2, 0), coarse_count - 1)
        high = min(max((i - 1) // 2 + 1, 0), coarse_count - 1)
        fraction = 0.75 if i % 2 == 0 else 0.25
        rows[i, low] += 1.0 - fraction
        rows[i, high] += fraction
    return rows


def interp_matrix():
    rows_x, rows_y = interp_rows(TILE_X), interp_rows(TILE_Y)
    whole = rows_x[:, None, None, :] * rows_y[None, :, :, None]
    return whole.reshape(TILE_X * TILE_Y, COARSE)


def rolled(x, by):
    by = by % x.shape[1]
    return x if by == 0 else pltpu.roll(x, by, 1)


def split(x):
    high = x.astype(BF16)
    return high, (x - high.astype(F32)).astype(BF16)


def kernel(
    n_mem, n_tile,
    pert_hbm, weight_ref, innov_ref, obsw_ref, static_ref, mask_ref, kx_ref, ky_ref, down_ref, up_ref,
    out_ref,
    pert, obs, ana, gbuf, part, rsbuf, gfull, alpha_hi, alpha_lo, coarse, smooth, fine,
    kxb, kyb, sendbuf, halo,
    pert_sem, ag_send, ag_recv, rs_send, rs_recv, halo_send, halo_recv,
):
    members, nvar, levels, cols = pert.shape
    own_levels = innov_ref.shape[1]
    n_group = levels // GROUP_LEVELS
    owners = GROUP_LEVELS // own_levels
    rows = members * GROUP_LEVELS
    packs = COARSE_X // 2
    prow = rows // packs
    grid_x = n_tile // GRID_Y
    me = lax.axis_index("mem")
    tile = lax.axis_index("tile")
    place_y = lax.rem(tile, GRID_Y)
    next_x = lax.rem(tile + GRID_Y, n_tile)
    prev_x = lax.rem(tile + n_tile - GRID_Y, n_tile)
    has_prev = place_y > 0
    has_next = place_y < GRID_Y - 1

    load = pltpu.make_async_copy(pert_hbm, pert, pert_sem)
    load.start()

    barrier = pltpu.get_barrier_semaphore()

    def greet(device_id):
        pl.semaphore_signal(barrier, inc=1, device_id=device_id, device_id_type=MESH)

    for i in range(1, n_mem):
        greet((lax.rem(me + i, n_mem), tile))
    greet((me, next_x))
    if grid_x > 2:
        greet((me, prev_x))

    greet((me, tile - place_y + lax.rem(place_y + GRID_Y - 1, GRID_Y)))
    greet((me, tile - place_y + lax.rem(place_y + 1, GRID_Y)))

    mask = mask_ref[...].astype(F32)
    for v in range(nvar):
        for l in range(own_levels):
            obs[v, l : l + 1, :] = mask * obsw_ref[v, l]
    ana[...] = jnp.zeros_like(ana)
    gbuf[0, me] = obs[...] * (ana[...] - innov_ref[...])

    pl.semaphore_wait(barrier, n_mem - 1 + min(grid_x - 1, 2) + 2)

    def gather_to(step, i):
        return pltpu.make_async_remote_copy(
            src_ref=gbuf.at[step, me], dst_ref=gbuf.at[step, me],
            send_sem=ag_send.at[step, i], recv_sem=ag_recv.at[step, me],
            device_id=(lax.rem(me + i, n_mem), tile), device_id_type=MESH,
        )

    def gathered_from(step, owner):
        return pltpu.make_async_remote_copy(
            src_ref=gbuf.at[step, owner], dst_ref=gbuf.at[step, owner],
            send_sem=ag_send.at[step, 0], recv_sem=ag_recv.at[step, owner],
            device_id=(owner, tile), device_id_type=MESH,
        )

    def reduce_to(step, owner):
        return pltpu.make_async_remote_copy(
            src_ref=part.at[step, owner], dst_ref=rsbuf.at[step, me],
            send_sem=rs_send.at[step, owner], recv_sem=rs_recv.at[step, me],
            device_id=(owner, tile), device_id_type=MESH,
        )

    def reduced_from(step, source):
        return pltpu.make_async_remote_copy(
            src_ref=part.at[step, source], dst_ref=rsbuf.at[step, source],
            send_sem=rs_send.at[step, source], recv_sem=rs_recv.at[step, source],
            device_id=(source, tile), device_id_type=MESH,
        )

    def halo_copy(step, group, way, side):
        target = ((tile + 1, tile - 1), (next_x, prev_x))[way][side]
        return pltpu.make_async_remote_copy(
            src_ref=sendbuf.at[step, group, way, side], dst_ref=halo.at[step, group, way, side],
            send_sem=halo_send.at[step, group, way, side],
            recv_sem=halo_recv.at[step, group, way, side],
            device_id=(me, target), device_id_type=MESH,
        )

    for i in range(1, n_mem):
        gather_to(0, i).start()

    for d in range(5):
        kxb[d] = jnp.broadcast_to(kx_ref[:, d : d + 1], (levels, COARSE))
        kyb[d] = jnp.broadcast_to(ky_ref[:, d : d + 1], (levels, COARSE))

    @pl.when(jnp.logical_not(has_prev))
    def _():
        for step in range(STEPS):
            for group in range(n_group):
                halo[step, group, 0, 0] = jnp.zeros((prow, COARSE), F32)

    @pl.when(jnp.logical_not(has_next))
    def _():
        for step in range(STEPS):
            for group in range(n_group):
                halo[step, group, 0, 1] = jnp.zeros((prow, COARSE), F32)

    lane = lax.broadcasted_iota(jnp.int32, (prow, COARSE), 1)
    index = (lane // COARSE_X, lane % COARSE_X)
    stride = (COARSE_X, 1)

    def pack(step, group, way):
        slot = index[way] // 2
        unit = 2 * stride[way]
        for side, source in ((0, (packs * 2 - 2) * stride[way]), (1, 0)):
            packed = None
            for q in range(packs):
                piece = coarse[group, q * prow : (q + 1) * prow, :]
                piece = rolled(piece, unit * q - source)
                packed = piece if packed is None else jnp.where(slot == q, piece, packed)
            sendbuf[step, group, way, side] = packed

    def convolve(step, group, way, q, weights):
        at, by = index[way], stride[way]
        count = packs * 2
        x = coarse[group, q * prow : (q + 1) * prow, :]
        before = rolled(halo[step, group, way, 0], -2 * by * q)
        after = rolled(halo[step, group, way, 1], (count - 2) * by - 2 * by * q)
        taps = (
            jnp.where(at < 2, before, rolled(x, 2 * by)),
            jnp.where(at < 1, rolled(before, -by), rolled(x, by)),
            x,
            jnp.where(at >= count - 1, rolled(after, by), rolled(x, -by)),
            jnp.where(at >= count - 2, after, rolled(x, -2 * by)),
        )
        total = None
        for d in range(5):
            k = weights[d, group * GROUP_LEVELS : (group + 1) * GROUP_LEVELS, :]
            k = jnp.concatenate([k] * (prow // GROUP_LEVELS), axis=0)
            total = k * taps[d] if total is None else total + k * taps[d]
        return total

    def project(step, group):
        for o in range(owners):
            owner = group * owners + o

            @pl.when(owner != me)
            def _():
                gathered_from(step, owner).wait_recv()

            for v in range(nvar):
                gfull[v, o * own_levels : (o + 1) * own_levels, :] = gbuf[step, owner, v]

        def one(j, carry):
            at = pl.ds(pl.multiple_of(j * LANES, LANES), LANES)
            g = [gfull[v, :, at] for v in range(nvar)]
            for k in range(members):
                total = None
                for v in range(nvar):
                    term = pert[k, v, group * GROUP_LEVELS : (group + 1) * GROUP_LEVELS, at].astype(F32) * g[v]
                    total = term if total is None else total + term
                high, low = split(total)
                alpha_hi[k * GROUP_LEVELS : (k + 1) * GROUP_LEVELS, at] = high
                alpha_lo[k * GROUP_LEVELS : (k + 1) * GROUP_LEVELS, at] = low
            return carry

        lax.fori_loop(0, cols // LANES, one, 0)
        coarse[group] = jnp.dot(
            alpha_hi[...], down_ref[...], preferred_element_type=F32
        ) + jnp.dot(alpha_lo[...], down_ref[...], preferred_element_type=F32)
        pack(step, group, 0)

        @pl.when(has_next)
        def _():
            halo_copy(step, group, 0, 0).start()

        @pl.when(has_prev)
        def _():
            halo_copy(step, group, 0, 1).start()

    def smooth_y(step, group):
        @pl.when(has_prev)
        def _():
            halo_copy(step, group, 0, 0).wait_recv()

        @pl.when(has_next)
        def _():
            halo_copy(step, group, 0, 1).wait_recv()

        for q in range(packs):
            done = convolve(step, group, 0, q, kyb)
            coarse[group, q * prow : (q + 1) * prow, :] = done
        pack(step, group, 1)
        halo_copy(step, group, 1, 0).start()
        halo_copy(step, group, 1, 1).start()

    def expand(step, group):
        halo_copy(step, group, 1, 0).wait_recv()
        halo_copy(step, group, 1, 1).wait_recv()
        each = prow // GROUP_LEVELS
        for q in range(packs):
            done = convolve(step, group, 1, q, kxb)
            factor = jnp.concatenate(
                [
                    jnp.full((GROUP_LEVELS, COARSE), weight_ref[q * each + m] * (1.0 / (n_mem * members)), F32)
                    for m in range(each)
                ],
                axis=0,
            )
            high, low = split(done * factor)
            smooth[q * prow : (q + 1) * prow, :COARSE] = high
            smooth[q * prow : (q + 1) * prow, COARSE:] = low
        fine[...] = jnp.dot(smooth[...], up_ref[...], preferred_element_type=F32)

        def one(j, carry):
            at = pl.ds(pl.multiple_of(j * LANES, LANES), LANES)
            total = [None] * nvar
            for k in range(members):
                f = fine[k * GROUP_LEVELS : (k + 1) * GROUP_LEVELS, at]
                for v in range(nvar):
                    term = pert[k, v, group * GROUP_LEVELS : (group + 1) * GROUP_LEVELS, at].astype(F32) * f
                    total[v] = term if total[v] is None else total[v] + term
            for o in range(owners):
                for v in range(nvar):
                    part[step, group * owners + o, v, :, at] = total[v][o * own_levels : (o + 1) * own_levels]
            return carry

        lax.fori_loop(0, cols // LANES, one, 0)
        for o in range(owners):
            owner = group * owners + o

            @pl.when(owner != me)
            def _():
                reduce_to(step, owner).start()

    def update(step, group):
        @pl.when(me // owners == group)
        def _():
            total = static_ref[...] * gbuf[step, me] + part[step, me]
            for i in range(1, n_mem):
                source = lax.rem(me + i, n_mem)
                reduced_from(step, source).wait_recv()
                total = total + rsbuf[step, source]
            now = ana[...]
            now = now - 0.5 * (now + total)
            if step == STEPS - 1:
                out_ref[...] = now
            else:
                ana[...] = now
                gbuf[step + 1, me] = obs[...] * (now - innov_ref[...])
                for i in range(1, n_mem):
                    gather_to(step + 1, i).start()

    load.wait()
    for step in range(STEPS):
        for stage in (project, smooth_y, expand, update):
            for group in range(n_group):
                stage(step, group)

    for step in range(STEPS):
        for i in range(1, n_mem):
            gather_to(step, i).wait_send()
        for owner in range(n_mem):

            @pl.when(owner != me)
            def _():
                reduce_to(step, owner).wait_send()

        for group in range(n_group):

            @pl.when(has_next)
            def _():
                halo_copy(step, group, 0, 0).wait_send()

            @pl.when(has_prev)
            def _():
                halo_copy(step, group, 0, 1).wait_send()

            halo_copy(step, group, 1, 0).wait_send()
            halo_copy(step, group, 1, 1).wait_send()


def body(n_mem, n_tile, perturbations, member_weight, innovation, obs_weight, static_var, obs_mask, kernel_x, kernel_y):
    members, nvar, levels, cols = perturbations.shape
    own = innovation.shape[1]
    n_group = levels // GROUP_LEVELS
    rows = members * GROUP_LEVELS
    prow = rows // (COARSE_X // 2)
    down = interp_matrix()
    down_b = jnp.asarray(down, BF16)
    up_b = jnp.asarray(np.concatenate([down.T, down.T], axis=0), BF16)
    vmem = pl.BlockSpec(memory_space=pltpu.VMEM)
    smem = pl.BlockSpec(memory_space=pltpu.SMEM)
    dma = pltpu.SemaphoreType.DMA
    return pl.pallas_call(
        functools.partial(kernel, n_mem, n_tile),
        out_shape=jax.ShapeDtypeStruct(innovation.shape, F32),
        in_specs=[pl.BlockSpec(memory_space=pl.ANY), smem, vmem, smem, vmem, vmem, vmem, vmem, vmem, vmem],
        out_specs=vmem,
        scratch_shapes=[
            pltpu.VMEM(perturbations.shape, BF16),
            pltpu.VMEM(innovation.shape, F32),
            pltpu.VMEM(innovation.shape, F32),
            pltpu.VMEM((STEPS, n_mem) + innovation.shape, F32),
            pltpu.VMEM((STEPS, n_mem) + innovation.shape, F32),
            pltpu.VMEM((STEPS, n_mem) + innovation.shape, F32),
            pltpu.VMEM((nvar, GROUP_LEVELS, cols), F32),
            pltpu.VMEM((rows, cols), BF16),
            pltpu.VMEM((rows, cols), BF16),
            pltpu.VMEM((n_group, rows, COARSE), F32),
            pltpu.VMEM((rows, 2 * COARSE), BF16),
            pltpu.VMEM((rows, cols), F32),
            pltpu.VMEM((5, levels, COARSE), F32),
            pltpu.VMEM((5, levels, COARSE), F32),
            pltpu.VMEM((STEPS, n_group, 2, 2, prow, COARSE), F32),
            pltpu.VMEM((STEPS, n_group, 2, 2, prow, COARSE), F32),
            dma,
            dma((STEPS, n_mem)),
            dma((STEPS, n_mem)),
            dma((STEPS, n_mem)),
            dma((STEPS, n_mem)),
            dma((STEPS, n_group, 2, 2)),
            dma((STEPS, n_group, 2, 2)),
        ],
        compiler_params=pltpu.CompilerParams(
            collective_id=0, has_side_effects=True, vmem_limit_bytes=48 * 1024 * 1024
        ),
    )(
        perturbations, member_weight, innovation, obs_weight, static_var,
        obs_mask.reshape(1, cols), kernel_x, kernel_y, down_b, up_b,
    )


def solution(mesh):
    placed = (
        P("mem", None, None, "tile"),
        P("mem"),
        P(None, "mem", "tile"),
        P(None, "mem"),
        P(None, "mem", "tile"),
        P("tile"),
        P(),
        P(),
    )
    return jax.shard_map(
        functools.partial(body, mesh.shape["mem"], mesh.shape["tile"]),
        mesh=mesh, in_specs=placed, out_specs=P(None, "mem", "tile"), check_vma=False,
    )
```

profile of v0, /device:TPU:7, one launch (start us, length us, event | category | flops | bytes accessed | tf_op | source)
XLA Modules:
  0.0 66.1 jit_solution(7816606345250425068)
XLA Ops:
  0.0 0.8 %copy.11.kx_ref = f32[32,5]{1,0:T(8,128)S(1)} copy(f32[32,5]{0,1:T(8,128)} %param.16) | data formatting | bytes 1280 | tf_op args[6]
  0.8 0.8 %copy.12.ky_ref = f32[32,5]{1,0:T(8,128)S(1)} copy(f32[32,5]{0,1:T(8,128)} %param.17) | data formatting | bytes 1280 | tf_op args[7]
  1.5 0.0 copy-start
  1.5 1.2 %copy-done = bf16[512,1024]{1,0:T(8,128)(2,1)S(1)} copy-done((bf16[512,1024]{1,0:T(8,128)(2,1)S(1)}, bf16[512,1024]{1,0:T(8,128)(2,1)}, u32[]{:S(2)}) %copy-start) | copy-done | bytes 1048600
  2.8 0.0 copy-start.1
  2.8 1.0 %copy-done.1 = bf16[1024,256]{1,0:T(8,128)(2,1)S(1)} copy-done((bf16[1024,256]{1,0:T(8,128)(2,1)S(1)}, bf16[1024,256]{1,0:T(8,128)(2,1)}, u32[]{:S(2)}) %copy-start.1) | copy-done | bytes 524312
  3.8 0.0 copy-start.2
  3.8 0.9 %copy-done.2 = f32[3,8,1024]{2,1,0:T(8,128)S(1)} copy-done((f32[3,8,1024]{2,1,0:T(8,128)S(1)}, f32[3,8,1024]{2,1,0:T(8,128)}, u32[]{:S(2)}) %copy-start.2) | copy-done | bytes 98328
  4.7 0.0 copy-start.3
  4.7 0.9 %copy-done.3 = f32[3,8,1024]{2,1,0:T(8,128)S(1)} copy-done((f32[3,8,1024]{2,1,0:T(8,128)S(1)}, f32[3,8,1024]{2,1,0:T(8,128)}, u32[]{:S(2)}) %copy-start.3) | copy-done | bytes 98328
  5.6 0.0 copy-start.4
  5.6 0.7 %copy-done.4 = s32[1024]{0:T(1024)S(1)} copy-done((s32[1024]{0:T(1024)S(1)}, s32[1024]{0:T(1024)}, u32[]{:S(2)}) %copy-start.4) | copy-done | bytes 4120
  6.3 0.0 copy-start.5
  6.3 0.7 %copy-done.5 = f32[3,8]{1,0:T(4,128)S(1)} copy-done((f32[3,8]{1,0:T(4,128)S(1)}, f32[3,8]{1,0:T(4,128)}, u32[]{:S(2)}) %copy-start.5) | copy-done | bytes 120
  7.0 0.0 copy-start.6
  7.0 0.7 copy-done.6
  7.6 57.9 %shard_map.100 = f32[3,8,1024]{2,1,0:T(8,128)S(1)} custom-call(bf16[24,3,32,1024]{3,2,1,0:T(8,128)(2,1)} %pert_hbm.1, f32[24]{0:T(128)S(1)} %copy-done.6, f32[3,8,1024]{2,1,0:T(8,128)S(1)} %copy-done.2, f32[3,8]{1,0:T(4,128)S(1)} %copy-done.5, f32[3,8,1024]{2,1,0:T(8,128)S(1)} %copy-done.3, s32[1,1024]{1,0:T(1,128)S(1)} %bitcast.1, ...), custom_call_target="tpu_custom_call" | custom-call | tf_op jit(solution)/shard_map/pallas_call | solution.py:346
  65.5 0.6 copy.14
Async XLA Ops:
  1.5 1.2 %copy-start = (bf16[512,1024]{1,0:T(8,128)(2,1)S(1)}, bf16[512,1024]{1,0:T(8,128)(2,1)}, u32[]{:S(2)}) copy-start(bf16[512,1024]{1,0:T(8,128)(2,1)} %constant.5.clone.up_ref) | copy-start | bytes 3145732
  2.8 1.0 %copy-start.1 = (bf16[1024,256]{1,0:T(8,128)(2,1)S(1)}, bf16[1024,256]{1,0:T(8,128)(2,1)}, u32[]{:S(2)}) copy-start(bf16[1024,256]{1,0:T(8,128)(2,1)} %constant.4.clone.down_ref) | copy-start | bytes 1572868
  3.8 0.9 %copy-start.2 = (f32[3,8,1024]{2,1,0:T(8,128)S(1)}, f32[3,8,1024]{2,1,0:T(8,128)}, u32[]{:S(2)}) copy-start(f32[3,8,1024]{2,1,0:T(8,128)} %innov_ref.1) | copy-start | bytes 294916
  4.7 0.9 %copy-start.3 = (f32[3,8,1024]{2,1,0:T(8,128)S(1)}, f32[3,8,1024]{2,1,0:T(8,128)}, u32[]{:S(2)}) copy-start(f32[3,8,1024]{2,1,0:T(8,128)} %static_ref.1) | copy-start | bytes 294916
  5.6 0.7 %copy-start.4 = (s32[1024]{0:T(1024)S(1)}, s32[1024]{0:T(1024)}, u32[]{:S(2)}) copy-start(s32[1024]{0:T(1024)} %param.15) | copy-start | bytes 12292
  6.3 0.7 %copy-start.5 = (f32[3,8]{1,0:T(4,128)S(1)}, f32[3,8]{1,0:T(4,128)}, u32[]{:S(2)}) copy-start(f32[3,8]{1,0:T(4,128)} %obsw_ref.1) | copy-start | bytes 292
  7.0 0.7 copy-start.6
where the time goes:
time: 66.5 us; the launch traced here: 66.1 us
  Pallas kernels  57.9 us (87%)
  local copies, waits for them, and re-layouts  8.25 us (12%)
    pallas_call x1, Pallas kernels, body(): pl.pallas_call(functools.partial(kernel, n_mem, n_tile), out_shape=jax.Sh...  57.9 us
    unnamed x17, local copies, waits for them, and re-layouts  8.25 us

commit v1 on v0

--- a/solution.py
+++ b/solution.py
@@ -15,7 +15,10 @@
 COARSE_X = TILE_X // 2
 COARSE_Y = TILE_Y // 2
 COARSE = COARSE_X * COARSE_Y
-GROUP_LEVELS = 16
+GROUP_LEVELS = 8
+DUE = (0.0, 2.4, 5.0, 11.0)
+PERIOD = 17.0
+PACE = 2.1
 LANES = 256
 MESH = pl.DeviceIdType.MESH
 F32 = jnp.float32
@@ -52,11 +55,12 @@
 
 def kernel(
     n_mem, n_tile,
-    pert_hbm, weight_ref, innov_ref, obsw_ref, static_ref, mask_ref, kx_ref, ky_ref, down_ref, up_ref,
+    pert_hbm, weight_hbm, innov_hbm, obsw_hbm, static_hbm, mask_hbm, kx_hbm, ky_hbm, down_hbm, up_hbm,
     out_ref,
+    weight_ref, innov_ref, obsw_ref, static_ref, mask_ref, kx_ref, ky_ref, down_ref, up_ref,
     pert, obs, ana, gbuf, part, rsbuf, gfull, alpha_hi, alpha_lo, coarse, smooth, fine,
     kxb, kyb, sendbuf, halo,
-    pert_sem, ag_send, ag_recv, rs_send, rs_recv, halo_send, halo_recv,
+    load_sem, ag_send, ag_recv, rs_send, rs_recv, halo_send, halo_recv,
 ):
     members, nvar, levels, cols = pert.shape
     own_levels = innov_ref.shape[1]
@@ -74,8 +78,14 @@
     has_prev = place_y > 0
     has_next = place_y < GRID_Y - 1
 
-    load = pltpu.make_async_copy(pert_hbm, pert, pert_sem)
-    load.start()
+    pairs = (
+        (innov_hbm, innov_ref), (mask_hbm, mask_ref), (obsw_hbm, obsw_ref),
+        (kx_hbm, kx_ref), (ky_hbm, ky_ref), (pert_hbm, pert), (down_hbm, down_ref),
+        (weight_hbm, weight_ref), (static_hbm, static_ref), (up_hbm, up_ref),
+    )
+    loads = [pltpu.make_async_copy(a, b, load_sem.at[i]) for i, (a, b) in enumerate(pairs)]
+    for load in loads:
+        load.start()
 
     barrier = pltpu.get_barrier_semaphore()
 
@@ -91,6 +101,8 @@
     greet((me, tile - place_y + lax.rem(place_y + GRID_Y - 1, GRID_Y)))
     greet((me, tile - place_y + lax.rem(place_y + 1, GRID_Y)))
 
+    for load in loads[:3]:
+        load.wait()
     mask = mask_ref[...].astype(F32)
     for v in range(nvar):
         for l in range(own_levels):
@@ -140,9 +152,14 @@
     for i in range(1, n_mem):
         gather_to(0, i).start()
 
-    for d in range(5):
-        kxb[d] = jnp.broadcast_to(kx_ref[:, d : d + 1], (levels, COARSE))
-        kyb[d] = jnp.broadcast_to(ky_ref[:, d : d + 1], (levels, COARSE))
+    for load in loads[3:5]:
+        load.wait()
+    shape = (levels, levels)
+    diagonal = lax.broadcasted_iota(jnp.int32, shape, 0) == lax.broadcasted_iota(jnp.int32, shape, 1)
+    for source, spread in ((kx_ref, kxb), (ky_ref, kyb)):
+        for d in range(5):
+            column = jnp.where(diagonal, jnp.broadcast_to(source[d : d + 1, :], shape), 0.0)
+            spread[d] = jnp.broadcast_to(jnp.sum(column, axis=1, keepdims=True), (levels, COARSE))
 
     @pl.when(jnp.logical_not(has_prev))
     def _():
@@ -302,11 +319,15 @@
                 for i in range(1, n_mem):
                     gather_to(step + 1, i).start()
 
-    load.wait()
-    for step in range(STEPS):
-        for stage in (project, smooth_y, expand, update):
-            for group in range(n_group):
-                stage(step, group)
+    for load in loads[5:]:
+        load.wait()
+    stages = (project, smooth_y, expand, update)
+    order = [
+        (PERIOD * step + DUE[i] + (1.0 if step == 0 and i < 2 else PACE) * group, group, step, i)
+        for step in range(STEPS) for i in range(len(stages)) for group in range(n_group)
+    ]
+    for _, group, step, i in sorted(order):
+        stages[i](step, group)
 
     for step in range(STEPS):
         for i in range(1, n_mem):
@@ -340,15 +361,22 @@
     down = interp_matrix()
     down_b = jnp.asarray(down, BF16)
     up_b = jnp.asarray(np.concatenate([down.T, down.T], axis=0), BF16)
-    vmem = pl.BlockSpec(memory_space=pltpu.VMEM)
-    smem = pl.BlockSpec(memory_space=pltpu.SMEM)
     dma = pltpu.SemaphoreType.DMA
     return pl.pallas_call(
         functools.partial(kernel, n_mem, n_tile),
         out_shape=jax.ShapeDtypeStruct(innovation.shape, F32),
-        in_specs=[pl.BlockSpec(memory_space=pl.ANY), smem, vmem, smem, vmem, vmem, vmem, vmem, vmem, vmem],
-        out_specs=vmem,
+        in_specs=[pl.BlockSpec(memory_space=pl.ANY)] * 10,
+        out_specs=pl.BlockSpec(memory_space=pltpu.VMEM),
         scratch_shapes=[
+            pltpu.SMEM(member_weight.shape, F32),
+            pltpu.VMEM(innovation.shape, F32),
+            pltpu.SMEM(obs_weight.shape, F32),
+            pltpu.VMEM(innovation.shape, F32),
+            pltpu.VMEM((1, cols), jnp.int32),
+            pltpu.VMEM((5, levels), F32),
+            pltpu.VMEM((5, levels), F32),
+            pltpu.VMEM(down_b.shape, BF16),
+            pltpu.VMEM(up_b.shape, BF16),
             pltpu.VMEM(perturbations.shape, BF16),
             pltpu.VMEM(innovation.shape, F32),
             pltpu.VMEM(innovation.shape, F32),
@@ -365,7 +393,7 @@
             pltpu.VMEM((5, levels, COARSE), F32),
             pltpu.VMEM((STEPS, n_group, 2, 2, prow, COARSE), F32),
             pltpu.VMEM((STEPS, n_group, 2, 2, prow, COARSE), F32),
-            dma,
+            dma((10,)),
             dma((STEPS, n_mem)),
             dma((STEPS, n_mem)),
             dma((STEPS, n_mem)),
@@ -374,11 +402,11 @@
             dma((STEPS, n_group, 2, 2)),
         ],
         compiler_params=pltpu.CompilerParams(
-            collective_id=0, has_side_effects=True, vmem_limit_bytes=48 * 1024 * 1024
+            collective_id=0, has_side_effects=True
         ),
     )(
         perturbations, member_weight, innovation, obs_weight, static_var,
-        obs_mask.reshape(1, cols), kernel_x, kernel_y, down_b, up_b,
+        obs_mask.reshape(1, cols), kernel_x.T, kernel_y.T, down_b, up_b,
     )
 
 

time: 66.5 us -> 58 us (0.87)
  the two profiles are of different devices: /device:TPU:7 before, /device:TPU:0 now
where the time goes in v1:
time: 58 us; the launch traced here: 57.9 us
  Pallas kernels  56.3 us (97%)
  local copies, waits for them, and re-layouts  1.54 us (3%)
    pallas_call x1, Pallas kernels, body(): pl.pallas_call(functools.partial(kernel, n_mem, n_tile), out_shape=jax.Sh...  56.3 us
    unnamed x1, local copies, waits for them, and re-layouts  1.54 us

profile of v1, /device:TPU:0, one launch (start us, length us, event | category | flops | bytes accessed | tf_op | source)
XLA Modules:
  0.0 57.9 jit_solution(15021699070927387788)
XLA Ops:
  0.0 56.3 %shard_map.100 = f32[3,8,1024]{2,1,0:T(8,128)} custom-call(bf16[24,3,32,1024]{3,2,1,0:T(8,128)(2,1)} %pert_hbm.1, f32[24]{0:T(128)} %weight_hbm.1, f32[3,8,1024]{2,1,0:T(8,128)} %innov_hbm.1, f32[3,8]{1,0:T(4,128)} %obsw_hbm.1, f32[3,8,1024]{2,1,0:T(8,128)} %static_hbm.1, s32[1,1024]{1,0:T(1,128)} %bitcast.3, f32[5,32]{1,0:T(8,128)} %bitcast.4, ...), custom_call_target="tpu_custom_call" | custom-call | tf_op jit(solution)/shard_map/pallas_call | solution.py:365
  56.3 1.5 %copy.12 = f32[3,8,1024]{2,1,0:T(8,128)} copy(f32[3,8,1024]{2,1,0:T(8,128)} %shard_map.100) | data formatting | bytes 196608

commit v2 on v1

--- a/solution.py
+++ b/solution.py
@@ -16,8 +16,8 @@
 COARSE_Y = TILE_Y // 2
 COARSE = COARSE_X * COARSE_Y
 GROUP_LEVELS = 8
-DUE = (0.0, 2.4, 5.0, 11.0)
-PERIOD = 17.0
+DUE = (0.0, 2.4, 5.0, 8.0)
+PERIOD = 11.0
 PACE = 2.1
 LANES = 256
 MESH = pl.DeviceIdType.MESH
@@ -58,9 +58,9 @@
     pert_hbm, weight_hbm, innov_hbm, obsw_hbm, static_hbm, mask_hbm, kx_hbm, ky_hbm, down_hbm, up_hbm,
     out_ref,
     weight_ref, innov_ref, obsw_ref, static_ref, mask_ref, kx_ref, ky_ref, down_ref, up_ref,
-    pert, obs, ana, gbuf, part, rsbuf, gfull, alpha_hi, alpha_lo, coarse, smooth, fine,
+    pert, obs, fields, ana, gbuf, part, rsbuf, gcols, pcols, rscols, gfull, alpha_hi, alpha_lo, coarse, smooth, fine,
     kxb, kyb, sendbuf, halo,
-    load_sem, ag_send, ag_recv, rs_send, rs_recv, halo_send, halo_recv,
+    load_sem, field_send, field_recv, ag_send, ag_recv, rs_send, rs_recv, agc_send, agc_recv, rsc_send, rsc_recv, halo_send, halo_recv,
 ):
     members, nvar, levels, cols = pert.shape
     own_levels = innov_ref.shape[1]
@@ -70,6 +70,8 @@
     packs = COARSE_X // 2
     prow = rows // packs
     grid_x = n_tile // GRID_Y
+    blocks = min(n_mem, cols // 128)
+    width = cols // blocks
     me = lax.axis_index("mem")
     tile = lax.axis_index("tile")
     place_y = lax.rem(tile, GRID_Y)
@@ -107,38 +109,59 @@
     for v in range(nvar):
         for l in range(own_levels):
             obs[v, l : l + 1, :] = mask * obsw_ref[v, l]
-    ana[...] = jnp.zeros_like(ana)
-    gbuf[0, me] = obs[...] * (ana[...] - innov_ref[...])
+    gbuf[me] = obs[...] * (0.0 - innov_ref[...])
 
     pl.semaphore_wait(barrier, n_mem - 1 + min(grid_x - 1, 2) + 2)
 
-    def gather_to(step, i):
+    def columns(block):
+        return pl.ds(pl.multiple_of(block * width, 128), width)
+
+    def remote(source, target, send, receive, member):
         return pltpu.make_async_remote_copy(
-            src_ref=gbuf.at[step, me], dst_ref=gbuf.at[step, me],
-            send_sem=ag_send.at[step, i], recv_sem=ag_recv.at[step, me],
-            device_id=(lax.rem(me + i, n_mem), tile), device_id_type=MESH,
+            src_ref=source, dst_ref=target, send_sem=send, recv_sem=receive,
+            device_id=(member, tile), device_id_type=MESH,
         )
 
-    def gathered_from(step, owner):
-        return pltpu.make_async_remote_copy(
-            src_ref=gbuf.at[step, owner], dst_ref=gbuf.at[step, owner],
-            send_sem=ag_send.at[step, 0], recv_sem=ag_recv.at[step, owner],
-            device_id=(owner, tile), device_id_type=MESH,
+    def other(i):
+        return lax.rem(me + i, n_mem)
+
+    def each_block(do, mine=False):
+        for i in range(0 if mine else 1, n_mem):
+            if blocks == n_mem:
+                do(other(i))
+            else:
+                pl.when(other(i) < blocks)(functools.partial(do, other(i)))
+
+    def if_block(do):
+        if blocks == n_mem:
+            do()
+        else:
+            pl.when(me < blocks)(do)
+
+    def gather(owner, to):
+        return remote(gbuf.at[owner], gbuf.at[owner], ag_send.at[to], ag_recv.at[owner], to)
+
+    def field(f, owner, to):
+        source = (static_ref, obs)[f]
+        return remote(
+            source.at[:, :, columns(to)], fields.at[f, owner],
+            field_send.at[f, to], field_recv.at[f, owner], to,
         )
 
-    def reduce_to(step, owner):
-        return pltpu.make_async_remote_copy(
-            src_ref=part.at[step, owner], dst_ref=rsbuf.at[step, me],
-            send_sem=rs_send.at[step, owner], recv_sem=rs_recv.at[step, me],
-            device_id=(owner, tile), device_id_type=MESH,
+    def reduce_columns(group, source, to):
+        return remote(
+            pcols.at[group, to], rscols.at[group, source],
+            rsc_send.at[group, to], rsc_recv.at[group, source], to,
         )
 
-    def reduced_from(step, source):
-        return pltpu.make_async_remote_copy(
-            src_ref=part.at[step, source], dst_ref=rsbuf.at[step, source],
-            send_sem=rs_send.at[step, source], recv_sem=rs_recv.at[step, source],
-            device_id=(source, tile), device_id_type=MESH,
+    def gather_columns(group, block, to):
+        return remote(
+            gcols.at[group, block], gcols.at[group, block],
+            agc_send.at[group, to], agc_recv.at[group, block], to,
         )
+
+    def reduce_levels(source, to):
+        return remote(part.at[to], rsbuf.at[source], rs_send.at[to], rs_recv.at[source], to)
 
     def halo_copy(step, group, way, side):
         target = ((tile + 1, tile - 1), (next_x, prev_x))[way][side]
@@ -150,7 +173,20 @@
         )
 
     for i in range(1, n_mem):
-        gather_to(0, i).start()
+        gather(me, other(i)).start()
+    loads[8].wait()
+
+    def send_fields(to):
+        for f in range(2):
+            field(f, me, to).start()
+
+    each_block(send_fields)
+
+    def keep_fields():
+        fields[0, me] = static_ref[:, :, columns(me)]
+        fields[1, me] = obs[:, :, columns(me)]
+
+    if_block(keep_fields)
 
     for load in loads[3:5]:
         load.wait()
@@ -208,20 +244,28 @@
             total = k * taps[d] if total is None else total + k * taps[d]
         return total
 
+    def of_group(f, group, v):
+        return jnp.concatenate([fields[f, group * owners + o, v] for o in range(owners)], axis=0)
+
     def project(step, group):
-        for o in range(owners):
-            owner = group * owners + o
-
-            @pl.when(owner != me)
-            def _():
-                gathered_from(step, owner).wait_recv()
-
-            for v in range(nvar):
-                gfull[v, o * own_levels : (o + 1) * own_levels, :] = gbuf[step, owner, v]
+        if step == 0:
+            for o in range(owners):
+                owner = group * owners + o
+
+                @pl.when(owner != me)
+                def _():
+                    gather(owner, owner).wait_recv()
+
+                for v in range(nvar):
+                    gfull[group, v, o * own_levels : (o + 1) * own_levels, :] = gbuf[owner, v]
+        else:
+            each_block(lambda block: gather_columns(group, block, block).wait_recv())
+            for block in range(blocks):
+                gfull[group, :, :, block * width : (block + 1) * width] = gcols[group, block]
 
         def one(j, carry):
             at = pl.ds(pl.multiple_of(j * LANES, LANES), LANES)
-            g = [gfull[v, :, at] for v in range(nvar)]
+            g = [gfull[group, v, :, at] for v in range(nvar)]
             for k in range(members):
                 total = None
                 for v in range(nvar):
@@ -288,56 +332,103 @@
                 for v in range(nvar):
                     term = pert[k, v, group * GROUP_LEVELS : (group + 1) * GROUP_LEVELS, at].astype(F32) * f
                     total[v] = term if total[v] is None else total[v] + term
-            for o in range(owners):
+            if step == 0:
                 for v in range(nvar):
-                    part[step, group * owners + o, v, :, at] = total[v][o * own_levels : (o + 1) * own_levels]
+                    for b in range(LANES // chunk):
+                        piece = total[v][:, b * chunk : (b + 1) * chunk]
+                        block = j * LANES // width if chunk == LANES else j * (LANES // chunk) + b
+                        inside = j * LANES % width if chunk == LANES else 0
+                        pcols[group, block, v, :, pl.ds(pl.multiple_of(inside, 128), chunk)] = piece
+            else:
+                for o in range(owners):
+                    for v in range(nvar):
+                        part[group * owners + o, v, :, at] = total[v][o * own_levels : (o + 1) * own_levels]
             return carry
 
+        chunk = min(LANES, width)
         lax.fori_loop(0, cols // LANES, one, 0)
+        if step == 0:
+            each_block(lambda block: reduce_columns(group, me, block).start())
+            return
+
+        def add_rest():
+            for v in range(nvar):
+                rest = of_group(0, group, v) * gcols[group, me, v] - ana[group, v]
+                for o in range(owners):
+                    part[group * owners + o, v, :, columns(me)] += rest[o * own_levels : (o + 1) * own_levels]
+
+        if_block(add_rest)
         for o in range(owners):
             owner = group * owners + o
 
             @pl.when(owner != me)
             def _():
-                reduce_to(step, owner).start()
+                reduce_levels(me, owner).start()
 
     def update(step, group):
-        @pl.when(me // owners == group)
-        def _():
-            total = static_ref[...] * gbuf[step, me] + part[step, me]
-            for i in range(1, n_mem):
-                source = lax.rem(me + i, n_mem)
-                reduced_from(step, source).wait_recv()
-                total = total + rsbuf[step, source]
-            now = ana[...]
-            now = now - 0.5 * (now + total)
-            if step == STEPS - 1:
-                out_ref[...] = now
-            else:
-                ana[...] = now
-                gbuf[step + 1, me] = obs[...] * (now - innov_ref[...])
+        if step == 0:
+            def by_columns():
+                for o in range(owners):
+                    owner = group * owners + o
+
+                    @pl.when(owner != me)
+                    def _():
+                        field(0, owner, owner).wait_recv()
+                        field(1, owner, owner).wait_recv()
+
                 for i in range(1, n_mem):
-                    gather_to(step + 1, i).start()
-
-    for load in loads[5:]:
+                    reduce_columns(group, other(i), other(i)).wait_recv()
+                for v in range(nvar):
+                    before = gfull[group, v, :, columns(me)]
+                    total = of_group(0, group, v) * before + pcols[group, me, v]
+                    for i in range(1, n_mem):
+                        total = total + rscols[group, other(i), v]
+                    now = -0.5 * total
+                    ana[group, v] = now
+                    gcols[group, me, v] = of_group(1, group, v) * now + before
+                for i in range(1, n_mem):
+                    gather_columns(group, me, other(i)).start()
+
+            if_block(by_columns)
+        else:
+
+            @pl.when(me // owners == group)
+            def _():
+                total = part[me]
+                for i in range(1, n_mem):
+                    reduce_levels(other(i), other(i)).wait_recv()
+                    total = total + rsbuf[other(i)]
+                out_ref[...] = -0.5 * total
+
+    for load in loads[5:8] + loads[9:]:
         load.wait()
     stages = (project, smooth_y, expand, update)
     order = [
-        (PERIOD * step + DUE[i] + (1.0 if step == 0 and i < 2 else PACE) * group, group, step, i)
+        (PERIOD * step + DUE[i] + (1.0 if step == 0 and i < 2 else PACE) * group + 4.0 * (step * i // 3), group, step, i)
         for step in range(STEPS) for i in range(len(stages)) for group in range(n_group)
     ]
     for _, group, step, i in sorted(order):
         stages[i](step, group)
 
+    for i in range(1, n_mem):
+        gather(me, other(i)).wait_send()
+        reduce_levels(me, other(i)).wait_send()
+
+    def sent(to):
+        for f in range(2):
+            field(f, me, to).wait_send()
+        for group in range(n_group):
+            reduce_columns(group, me, to).wait_send()
+
+    each_block(sent)
+
+    def sent_columns():
+        for i in range(1, n_mem):
+            for group in range(n_group):
+                gather_columns(group, me, other(i)).wait_send()
+
+    if_block(sent_columns)
     for step in range(STEPS):
-        for i in range(1, n_mem):
-            gather_to(step, i).wait_send()
-        for owner in range(n_mem):
-
-            @pl.when(owner != me)
-            def _():
-                reduce_to(step, owner).wait_send()
-
         for group in range(n_group):
 
             @pl.when(has_next)
@@ -358,6 +449,8 @@
     n_group = levels // GROUP_LEVELS
     rows = members * GROUP_LEVELS
     prow = rows // (COARSE_X // 2)
+    blocks = min(n_mem, cols // 128)
+    width = cols // blocks
     down = interp_matrix()
     down_b = jnp.asarray(down, BF16)
     up_b = jnp.asarray(np.concatenate([down.T, down.T], axis=0), BF16)
@@ -379,11 +472,15 @@
             pltpu.VMEM(up_b.shape, BF16),
             pltpu.VMEM(perturbations.shape, BF16),
             pltpu.VMEM(innovation.shape, F32),
-            pltpu.VMEM(innovation.shape, F32),
-            pltpu.VMEM((STEPS, n_mem) + innovation.shape, F32),
-            pltpu.VMEM((STEPS, n_mem) + innovation.shape, F32),
-            pltpu.VMEM((STEPS, n_mem) + innovation.shape, F32),
-            pltpu.VMEM((nvar, GROUP_LEVELS, cols), F32),
+            pltpu.VMEM((2, n_mem, nvar, own, width), F32),
+            pltpu.VMEM((n_group, nvar, GROUP_LEVELS, width), F32),
+            pltpu.VMEM((n_mem,) + innovation.shape, F32),
+            pltpu.VMEM((n_mem,) + innovation.shape, F32),
+            pltpu.VMEM((n_mem,) + innovation.shape, F32),
+            pltpu.VMEM((n_group, blocks, nvar, GROUP_LEVELS, width), F32),
+            pltpu.VMEM((n_group, blocks, nvar, GROUP_LEVELS, width), F32),
+            pltpu.VMEM((n_group, n_mem, nvar, GROUP_LEVELS, width), F32),
+            pltpu.VMEM((n_group, nvar, GROUP_LEVELS, cols), F32),
             pltpu.VMEM((rows, cols), BF16),
             pltpu.VMEM((rows, cols), BF16),
             pltpu.VMEM((n_group, rows, COARSE), F32),
@@ -394,10 +491,16 @@
             pltpu.VMEM((STEPS, n_group, 2, 2, prow, COARSE), F32),
             pltpu.VMEM((STEPS, n_group, 2, 2, prow, COARSE), F32),
             dma((10,)),
-            dma((STEPS, n_mem)),
-            dma((STEPS, n_mem)),
-            dma((STEPS, n_mem)),
-            dma((STEPS, n_mem)),
+            dma((2, n_mem)),
+            dma((2, n_mem)),
+            dma((n_mem,)),
+            dma((n_mem,)),
+            dma((n_mem,)),
+            dma((n_mem,)),
+            dma((n_group, n_mem)),
+            dma((n_group, n_mem)),
+            dma((n_group, n_mem)),
+            dma((n_group, n_mem)),
             dma((STEPS, n_group, 2, 2)),
             dma((STEPS, n_group, 2, 2)),
         ],

time: 58 us -> 57.3 us (0.988)
  the two profiles are of different devices: /device:TPU:0 before, /device:TPU:7 now
where the time goes in v2:
time: 57.3 us; the launch traced here: 57.2 us
  Pallas kernels  55.6 us (97%)
  local copies, waits for them, and re-layouts  1.54 us (3%)
    pallas_call x1, Pallas kernels, body(): pl.pallas_call(functools.partial(kernel, n_mem, n_tile), out_shape=jax.Sh...  55.6 us
    unnamed x1, local copies, waits for them, and re-layouts  1.54 us

profile of v2, /device:TPU:7, one launch (start us, length us, event | category | flops | bytes accessed | tf_op | source)
XLA Modules:
  0.0 57.2 jit_solution(5101931933244104411)
XLA Ops:
  0.0 55.6 %shard_map.100 = f32[3,8,1024]{2,1,0:T(8,128)} custom-call(bf16[24,3,32,1024]{3,2,1,0:T(8,128)(2,1)} %pert_hbm.1, f32[24]{0:T(128)} %weight_hbm.1, f32[3,8,1024]{2,1,0:T(8,128)} %innov_hbm.1, f32[3,8]{1,0:T(4,128)} %obsw_hbm.1, f32[3,8,1024]{2,1,0:T(8,128)} %static_hbm.1, s32[1,1024]{1,0:T(1,128)} %bitcast.3, f32[5,32]{1,0:T(8,128)} %bitcast.4, ...), custom_call_target="tpu_custom_call" | custom-call | tf_op jit(solution)/shard_map/pallas_call | solution.py:458
  55.6 1.5 %copy.12 = f32[3,8,1024]{2,1,0:T(8,128)} copy(f32[3,8,1024]{2,1,0:T(8,128)} %shard_map.100) | data formatting | bytes 196608

commit v3 on v2

--- a/solution.py
+++ b/solution.py
@@ -16,8 +16,8 @@
 COARSE_Y = TILE_Y // 2
 COARSE = COARSE_X * COARSE_Y
 GROUP_LEVELS = 8
-DUE = (0.0, 2.4, 5.0, 8.0)
-PERIOD = 11.0
+DUE = (0.0, 100.0, 200.0, 300.0)
+PERIOD = 1000.0
 PACE = 2.1
 LANES = 256
 MESH = pl.DeviceIdType.MESH

time: 57.3 us -> 55 us (0.960)
  Pallas kernels: 55.6 us -> 53.3 us
    pallas_call x1, Pallas kernels: 55.6 us -> 53.3 us  [body(): pl.pallas_call(functools.partial(kernel, n_mem, n_tile), out_shape=jax.Sh...]
where the time goes in v3:
time: 55 us; the launch traced here: 54.9 us
  Pallas kernels  53.3 us (97%)
  local copies, waits for them, and re-layouts  1.54 us (3%)
    pallas_call x1, Pallas kernels, body(): pl.pallas_call(functools.partial(kernel, n_mem, n_tile), out_shape=jax.Sh...  53.3 us
    unnamed x1, local copies, waits for them, and re-layouts  1.54 us

profile of v3, /device:TPU:7, one launch (start us, length us, event | category | flops | bytes accessed | tf_op | source)
XLA Modules:
  0.0 54.9 jit_solution(14372418392178428986)
XLA Ops:
  0.0 53.3 %shard_map.100 = f32[3,8,1024]{2,1,0:T(8,128)} custom-call(bf16[24,3,32,1024]{3,2,1,0:T(8,128)(2,1)} %pert_hbm.1, f32[24]{0:T(128)} %weight_hbm.1, f32[3,8,1024]{2,1,0:T(8,128)} %innov_hbm.1, f32[3,8]{1,0:T(4,128)} %obsw_hbm.1, f32[3,8,1024]{2,1,0:T(8,128)} %static_hbm.1, s32[1,1024]{1,0:T(1,128)} %bitcast.3, f32[5,32]{1,0:T(8,128)} %bitcast.4, ...), custom_call_target="tpu_custom_call" | custom-call | tf_op jit(solution)/shard_map/pallas_call | solution.py:458
  53.3 1.5 %copy.12 = f32[3,8,1024]{2,1,0:T(8,128)} copy(f32[3,8,1024]{2,1,0:T(8,128)} %shard_map.100) | data formatting | bytes 196608
